TPU v7x, 32 devices: a whole 2x2x4 slice. The times are simulated.
32 devices in a mesh: dp: 4 (over z), expert: 8 (over y, x, core).
Axes of the slice: x: 2, y: 2, z: 4, core: 2. Of those that a mesh axis runs over, the one named last changes fastest.
Arguments:
- tokens: bfloat16 [8192, 768], P(('dp', 'expert')), may hold values from -6 to 6
- segment_ids: int32 [32, 256], P(('dp', 'expert')), may hold values from 0 to 2, never falling along the last dimension, each value on 1 to 204 neighbouring positions
- routes: int32 [8192, 2], P(('dp', 'expert')), may hold values from 0 to 15, all different within a row
- ln1_gain: float32 [768], P('dp'), may hold values from 0.5 to 1.5
- ln1_bias: float32 [768], P('dp'), may hold values from -0.6 to 0.6
- ln2_gain: float32 [768], P('dp'), may hold values from 0.5 to 1.5
- ln2_bias: float32 [768], P('dp'), may hold values from -0.6 to 0.6
- w_query: float32 [768, 768], P('dp'), may hold values from -0.3125 to 0.3125
- w_key: float32 [768, 768], P('dp'), may hold values from -0.3125 to 0.3125
- w_value: float32 [768, 768], P('dp'), may hold values from -0.21875 to 0.21875
- w_output: float32 [768, 768], P('dp'), may hold values from -0.875 to 0.875
- w_router: float32 [768, 16], P('dp'), may hold values from -0.15625 to 0.15625
- frozen_in: float32 [8, 768, 3072], P('expert', 'dp'), may hold values from -0.21875 to 0.21875
- frozen_out: float32 [8, 3072, 768], P('expert', 'dp'), may hold values from -0.1875 to 0.1875
- new_in: float32 [8, 768, 3072], P('expert', 'dp'), may hold values from -0.21875 to 0.21875
- new_out: float32 [8, 3072, 768], P('expert', 'dp'), may hold values from -0.1875 to 0.1875
- cotangent: bfloat16 [8192, 768], P(('dp', 'expert')), may hold values from -6 to 6
Outputs:
- block_out: bfloat16 [8192, 768], P(('dp', 'expert'))
- grad_tokens: bfloat16 [8192, 768], P(('dp', 'expert'))
- grad_w_query: float32 [768, 768], P('dp')
- grad_w_key: float32 [768, 768], P('dp')
- grad_w_value: float32 [768, 768], P('dp')
- grad_w_output: float32 [768, 768], P('dp')
- grad_w_router: float32 [768, 16], P('dp')
- grad_ln1_gain: float32 [768], P('dp')
- grad_ln1_bias: float32 [768], P('dp')
- grad_ln2_gain: float32 [768], P('dp')
- grad_ln2_bias: float32 [768], P('dp')
- grad_new_in: float32 [8, 768, 3072], P('expert', 'dp')
- grad_new_out: float32 [8, 3072, 768], P('expert', 'dp')
Inputs may be any that keep to these rules, and one draw needn't show every extreme that they name: `segment_ids`: within each row ids never fall, every sequence has 1 to 204 tokens, and one has exactly 204. `routes`: the two experts of a token differ.
All inputs are finite; a program needn't handle non-finite values.
Results may differ from a plain program's by a relative error of at most 0.014.
The roundings to bfloat16 on the way count: a program that leaves them out, or rounds other values in their place, can miss the bound.
Values may be sent and summed in bfloat16 or wider, within the bound.
A program may use at most 192 MiB of HBM per device.

v0:
```python
import jax
import jax.numpy as jnp
from jax import lax
from jax.sharding import PartitionSpec as P

HEADS = 12
HEAD = 64
NORM_EPS = 1e-05
MASKED = -1e30


def layer_norm(values, norm_gain, norm_shift):
    average = jnp.mean(values, axis=-1, keepdims=True)
    centred = values - average
    variance = jnp.mean(centred * centred, axis=-1, keepdims=True)
    return centred * lax.rsqrt(variance + NORM_EPS) * norm_gain + norm_shift


def inner_rows(left, right):
    return lax.dot_general(
        left, right, (((0,), (0,)), ((), ())), preferred_element_type=jnp.float32
    )


def times_transposed(left, right):
    return lax.dot_general(
        left, right, (((1,), (1,)), ((), ())), preferred_element_type=jnp.float32
    )


def shards(
    tokens,
    segment_ids,
    routes,
    ln1_gain,
    ln1_bias,
    ln2_gain,
    ln2_bias,
    w_query,
    w_key,
    w_value,
    w_output,
    w_router,
    frozen_in,
    frozen_out,
    new_in,
    new_out,
    cotangent,
):
    row_count = tokens.shape[0]
    model_width = tokens.shape[1]
    expert_count = w_router.shape[1]
    owner_count = expert_count // 2
    capacity = 5 * row_count // (2 * expert_count)
    slot_count = expert_count * capacity
    score_scale = HEAD ** (-0.5)
    (
        full_query,
        full_key,
        full_value,
        full_output,
        full_router,
        gain_one,
        bias_one,
        gain_two,
        bias_two,
    ) = (
        lax.all_gather(w_query.astype(jnp.bfloat16), "dp", axis=0, tiled=True),
        lax.all_gather(w_key.astype(jnp.bfloat16), "dp", axis=0, tiled=True),
        lax.all_gather(w_value.astype(jnp.bfloat16), "dp", axis=0, tiled=True),
        lax.all_gather(w_output.astype(jnp.bfloat16), "dp", axis=0, tiled=True),
        lax.all_gather(w_router.astype(jnp.bfloat16), "dp", axis=0, tiled=True),
        lax.all_gather(ln1_gain.astype(jnp.bfloat16), "dp", axis=0, tiled=True),
        lax.all_gather(ln1_bias.astype(jnp.bfloat16), "dp", axis=0, tiled=True),
        lax.all_gather(ln2_gain.astype(jnp.bfloat16), "dp", axis=0, tiled=True),
        lax.all_gather(ln2_bias.astype(jnp.bfloat16), "dp", axis=0, tiled=True),
    )
    full_frozen_in, full_frozen_out, full_new_in, full_new_out = (
        lax.all_gather(frozen_in[0].astype(jnp.bfloat16), "dp", axis=0, tiled=True),
        lax.all_gather(frozen_out[0].astype(jnp.bfloat16), "dp", axis=0, tiled=True),
        lax.all_gather(new_in[0].astype(jnp.bfloat16), "dp", axis=0, tiled=True),
        lax.all_gather(new_out[0].astype(jnp.bfloat16), "dp", axis=0, tiled=True),
    )
    stack_in = jnp.stack([full_frozen_in, full_new_in])
    stack_out = jnp.stack([full_frozen_out, full_new_out])
    gain_one_f = gain_one.astype(jnp.float32)
    bias_one_f = bias_one.astype(jnp.float32)
    gain_two_f = gain_two.astype(jnp.float32)
    bias_two_f = bias_two.astype(jnp.float32)
    rows_float = tokens.astype(jnp.float32)
    act_one = layer_norm(rows_float, gain_one_f, bias_one_f).astype(jnp.bfloat16)
    query_rows = jnp.dot(act_one, full_query, preferred_element_type=jnp.float32).astype(
        jnp.bfloat16
    )
    key_rows = jnp.dot(act_one, full_key, preferred_element_type=jnp.float32).astype(jnp.bfloat16)
    value_rows = jnp.dot(act_one, full_value, preferred_element_type=jnp.float32).astype(
        jnp.bfloat16
    )
    query_heads = query_rows.reshape(row_count, HEADS, HEAD)
    key_heads = key_rows.reshape(row_count, HEADS, HEAD)
    value_heads = value_rows.reshape(row_count, HEADS, HEAD)
    segments = segment_ids[0]
    positions = jnp.arange(row_count, dtype=jnp.int32)

    def block_scores(block_index):
        lower = block_index * row_count
        upper_end = lower + row_count
        scores = (
            jnp.einsum("qhd,khd->hqk", query_heads, key_heads, preferred_element_type=jnp.float32)
            * score_scale
        )
        allowed = (segments[lower:upper_end, None] == segments[None, :upper_end]) & (
            positions[None, :upper_end] <= positions[lower:upper_end, None]
        )
        return (jnp.where(allowed[None], scores, MASKED), allowed)

    block_index = 0
    upper_end = (block_index + 1) * row_count
    scores, allowed = block_scores(block_index)
    row_max = jnp.max(scores, axis=-1, keepdims=True)
    expo = jnp.exp(scores - row_max)
    row_total = jnp.sum(expo, axis=-1, keepdims=True)
    probabilities = expo / row_total
    log_totals = [row_max + jnp.log(row_total)]
    attended_parts = jnp.einsum(
        "hqk,khd->qhd",
        probabilities.astype(jnp.bfloat16),
        value_heads,
        preferred_element_type=jnp.float32,
    )
    attended = attended_parts.reshape(row_count, model_width).astype(jnp.bfloat16)
    residual = rows_float + jnp.dot(attended, full_output, preferred_element_type=jnp.float32)
    normed_two = layer_norm(residual, gain_two_f, bias_two_f)
    act_two = normed_two.astype(jnp.bfloat16)
    logits = jnp.dot(act_two, full_router, preferred_element_type=jnp.float32)
    expert_iota = jnp.arange(expert_count, dtype=jnp.int32)
    choose = (routes[:, :, None] == expert_iota[None, None, :]).astype(jnp.float32)
    picked = jnp.sum(choose * logits[:, None, :], axis=2)
    gate_values = jax.nn.softmax(picked, axis=-1)
    flat_ids = routes.reshape(2 * row_count)
    onehot = (flat_ids[:, None] == expert_iota[None, :]).astype(jnp.int32)
    running = jnp.cumsum(onehot, axis=0)
    position = jnp.sum(onehot * running, axis=1) - 1
    is_kept = position < capacity
    kept_float = is_kept.astype(jnp.float32)
    slot_index = (flat_ids % owner_count * 2 + flat_ids // owner_count) * capacity + position
    safe_slot = jnp.where(is_kept, slot_index, 0)
    pair_iota = jnp.arange(2 * row_count, dtype=jnp.int32)
    pair_of_slot = (
        jnp.full((slot_count + 1,), 2 * row_count, jnp.int32)
        .at[jnp.where(is_kept, slot_index, slot_count)]
        .set(pair_iota)[:slot_count]
    )
    token_of_slot = pair_of_slot // 2
    padded_act = jnp.concatenate([act_two, jnp.zeros((1, model_width), jnp.bfloat16)], axis=0)
    dispatched = padded_act[token_of_slot].reshape(owner_count, 2, capacity, model_width)
    received_rows = lax.all_to_all(dispatched, "expert", split_axis=0, concat_axis=0, tiled=True)
    pre_values = jnp.einsum(
        "sekd,edf->sekf", received_rows, stack_in, preferred_element_type=jnp.float32
    )
    hidden = jax.nn.gelu(pre_values).astype(jnp.bfloat16)
    produced_rows = jnp.einsum(
        "sekf,efd->sekd", hidden, stack_out, preferred_element_type=jnp.float32
    ).astype(jnp.bfloat16)
    returned = lax.all_to_all(
        produced_rows, "expert", split_axis=0, concat_axis=0, tiled=True
    ).reshape(slot_count, model_width)
    pair_out = returned[safe_slot].astype(jnp.float32)
    pair_weight = gate_values.reshape(2 * row_count) * kept_float
    mixture = jnp.sum((pair_out * pair_weight[:, None]).reshape(row_count, 2, model_width), axis=1)
    block_out = (residual + mixture).astype(jnp.bfloat16)
    d_out = cotangent.astype(jnp.float32)
    d_out_pairs = jnp.repeat(d_out, 2, axis=0)
    d_gate = kept_float * jnp.sum(pair_out * d_out_pairs, axis=1)
    slot_weight = jnp.concatenate([pair_weight, jnp.zeros((1,), jnp.float32)])[pair_of_slot]
    padded_grad = jnp.concatenate([d_out, jnp.zeros((1, model_width), jnp.float32)], axis=0)
    d_send = (
        (padded_grad[token_of_slot] * slot_weight[:, None])
        .astype(jnp.bfloat16)
        .reshape(owner_count, 2, capacity, model_width)
    )
    again_frozen_in, again_frozen_out, again_new_in, again_new_out = (
        lax.all_gather(frozen_in[0].astype(jnp.bfloat16), "dp", axis=0, tiled=True),
        lax.all_gather(frozen_out[0].astype(jnp.bfloat16), "dp", axis=0, tiled=True),
        lax.all_gather(new_in[0].astype(jnp.bfloat16), "dp", axis=0, tiled=True),
        lax.all_gather(new_out[0].astype(jnp.bfloat16), "dp", axis=0, tiled=True),
    )
    back_in = jnp.stack([again_frozen_in, again_new_in])
    back_out = jnp.stack([again_frozen_out, again_new_out])
    d_produced = lax.all_to_all(d_send, "expert", split_axis=0, concat_axis=0, tiled=True)
    d_hidden = jnp.einsum(
        "sekd,efd->sekf", d_produced, back_out, preferred_element_type=jnp.float32
    )
    gelu_value, gelu_back = jax.vjp(jax.nn.gelu, pre_values)
    d_pre = gelu_back(d_hidden)[0].astype(jnp.bfloat16)
    hidden_again = gelu_value.astype(jnp.bfloat16)
    d_received = jnp.einsum(
        "sekf,edf->sekd", d_pre, back_in, preferred_element_type=jnp.float32
    ).astype(jnp.bfloat16)
    grad_in_full = jnp.einsum(
        "skd,skf->df", received_rows[:, 1], d_pre[:, 1], preferred_element_type=jnp.float32
    )
    grad_out_full = jnp.einsum(
        "skf,skd->fd", hidden_again[:, 1], d_produced[:, 1], preferred_element_type=jnp.float32
    )
    grad_in_part, grad_out_part = (
        lax.psum_scatter(
            grad_in_full.astype(jnp.bfloat16), "dp", scatter_dimension=0, tiled=True
        ).astype(jnp.float32),
        lax.psum_scatter(
            grad_out_full.astype(jnp.bfloat16), "dp", scatter_dimension=0, tiled=True
        ).astype(jnp.float32),
    )
    d_returned = lax.all_to_all(
        d_received, "expert", split_axis=0, concat_axis=0, tiled=True
    ).reshape(slot_count, model_width)
    d_act_moe = jnp.sum(
        (d_returned[safe_slot].astype(jnp.float32) * kept_float[:, None]).reshape(
            row_count, 2, model_width
        ),
        axis=1,
    )
    d_gate_rows = d_gate.reshape(row_count, 2)
    d_picked = gate_values * (
        d_gate_rows - jnp.sum(gate_values * d_gate_rows, axis=1, keepdims=True)
    )
    d_logits = jnp.sum(choose * d_picked[:, :, None], axis=1).astype(jnp.bfloat16)
    grad_router = inner_rows(act_two, d_logits)
    d_act_two = d_act_moe + times_transposed(d_logits, full_router)
    norm_two_value, norm_two_back = jax.vjp(layer_norm, residual, gain_two_f, bias_two_f)
    d_resid_norm, grad_gain_two, grad_bias_two = norm_two_back(d_act_two)
    d_residual = d_out + d_resid_norm
    d_branch = d_residual.astype(jnp.bfloat16)
    grad_output = inner_rows(attended, d_branch)
    d_attended = (
        times_transposed(d_branch, full_output).astype(jnp.bfloat16).reshape(row_count, HEADS, HEAD)
    )
    block_index = 0
    lower = block_index * row_count
    upper_end = lower + row_count
    scores, allowed = block_scores(block_index)
    probabilities = jnp.exp(scores - log_totals[block_index])
    grad_probs = jnp.einsum(
        "qhd,khd->hqk", d_attended, value_heads, preferred_element_type=jnp.float32
    )
    row_delta = jnp.sum(grad_probs * probabilities, axis=-1, keepdims=True)
    grad_scores = jnp.where(allowed[None], probabilities * (grad_probs - row_delta), 0.0).astype(
        jnp.bfloat16
    )
    d_query_parts = (
        jnp.einsum("hqk,khd->qhd", grad_scores, key_heads, preferred_element_type=jnp.float32)
        * score_scale
    )
    d_key_sum = (
        jnp.einsum("hqk,qhd->khd", grad_scores, query_heads, preferred_element_type=jnp.float32)
        * score_scale
    )
    d_value_sum = jnp.einsum(
        "hqk,qhd->khd",
        probabilities.astype(jnp.bfloat16),
        d_attended,
        preferred_element_type=jnp.float32,
    )
    d_query = d_query_parts.reshape(row_count, model_width).astype(jnp.bfloat16)
    d_key = d_key_sum.reshape(row_count, model_width).astype(jnp.bfloat16)
    d_value = d_value_sum.reshape(row_count, model_width).astype(jnp.bfloat16)
    grad_query = inner_rows(act_one, d_query)
    grad_key = inner_rows(act_one, d_key)
    grad_value = inner_rows(act_one, d_value)
    d_act_one = (
        times_transposed(d_query, full_query)
        + times_transposed(d_key, full_key)
        + times_transposed(d_value, full_value)
    )
    norm_one_value, norm_one_back = jax.vjp(layer_norm, rows_float, gain_one_f, bias_one_f)
    d_rows_norm, grad_gain_one, grad_bias_one = norm_one_back(d_act_one)
    grad_tokens = (d_residual + d_rows_norm).astype(jnp.bfloat16)
    summed = lax.psum(
        (
            grad_query,
            grad_key,
            grad_value,
            grad_output,
            grad_router,
            grad_gain_one,
            grad_bias_one,
            grad_gain_two,
            grad_bias_two,
        ),
        ("dp", "expert"),
    )
    share_rows = model_width // lax.axis_size("dp")
    offset = lax.axis_index("dp") * share_rows
    shares = tuple((lax.dynamic_slice_in_dim(member, offset, share_rows, 0) for member in summed))
    return (
        block_out,
        grad_tokens,
        shares[0],
        shares[1],
        shares[2],
        shares[3],
        shares[4],
        shares[5],
        shares[6],
        shares[7],
        shares[8],
        grad_in_part[None],
        grad_out_part[None],
    )


def solution(mesh):
    in_specs = (
        P(("dp", "expert"), None),
        P(("dp", "expert"), None),
        P(("dp", "expert"), None),
        P("dp"),
        P("dp"),
        P("dp"),
        P("dp"),
        P("dp", None),
        P("dp", None),
        P("dp", None),
        P("dp", None),
        P("dp", None),
        P("expert", "dp", None),
        P("expert", "dp", None),
        P("expert", "dp", None),
        P("expert", "dp", None),
        P(("dp", "expert"), None),
    )
    out_specs = (
        P(("dp", "expert"), None),
        P(("dp", "expert"), None),
        P("dp", None),
        P("dp", None),
        P("dp", None),
        P("dp", None),
        P("dp", None),
        P("dp"),
        P("dp"),
        P("dp"),
        P("dp"),
        P("expert", "dp", None),
        P("expert", "dp", None),
    )
    return jax.shard_map(shards, mesh=mesh, in_specs=in_specs, out_specs=out_specs, check_vma=False)
```

profile of v0, /device:TPU:0, one launch (start us, length us, event | category | flops | bytes accessed | tf_op | source)
XLA Modules:
  0.0 1022.0 jit_solution(8854546606733937688)
XLA Ops:
  27.9 14.3 %all-reduce.8 = (bf16[768]{0:T(1024)(128)(2,1)S(1)}, bf16[768]{0:T(1024)(128)(2,1)S(1)}, bf16[768]{0:T(1024)(128)(2,1)S(1)}, bf16[768]{0:T(1024)(128)(2,1)S(1)}) all-reduce(bf16[768]{0:T(1024)(128)(2,1)S(1)} %dynamic-update-slice.1, bf16[768]{0:T(1024)(128)(2,1)S(1)} %dynamic-update-slice, ...), channel_id=1, replica_groups=mesh['dp'=4,'expert'=8] {'dp'}, use_global_device_ids=true, to_apply=%add.3 | all-reduce | flops 3072 | bytes 12288
  48.0 27.4 %all-gather.18.cloned.1.call-done = bf16[768,768]{1,0:T(8,128)(2,1)} async-done(((bf16[192,768]{1,0:T(8,128)(2,1)}), bf16[768,768]{1,0:T(8,128)(2,1)}) %all-gather.18.cloned.1.call-update) | async-done | bytes 1179664 | tf_op jit(solution)/shard_map/all_gather | solution.py:69
  77.4 29.7 %all-gather.16.cloned.1.call-done = bf16[768,768]{1,0:T(8,128)(2,1)} async-done(((bf16[192,768]{1,0:T(8,128)(2,1)}), bf16[768,768]{1,0:T(8,128)(2,1)}) %all-gather.16.cloned.1.call-update) | async-done | bytes 1179664 | tf_op jit(solution)/shard_map/all_gather | solution.py:68
  112.2 26.4 %all-gather.20.cloned.1.call-done = bf16[768,768]{1,0:T(8,128)(2,1)} async-done(((bf16[192,768]{1,0:T(8,128)(2,1)}), bf16[768,768]{1,0:T(8,128)(2,1)}) %all-gather.20.cloned.1.call-update) | async-done | bytes 1179664 | tf_op jit(solution)/shard_map/all_gather | solution.py:71
  145.6 18.3 %all_to_all.20 = bf16[8,2,40,768]{3,2,1,0:T(8,128)(2,1)S(1)} all-to-all(bf16[8,2,40,768]{3,2,1,0:T(8,128)(2,1)S(1)} %bitcast.156), channel_id=1, replica_groups=mesh['dp'=4,'expert'=8] {'expert'}, dimensions={0} | all-to-all | bytes 1966080 | tf_op jit(solution)/shard_map/all_to_all | solution.py:157
  163.8 65.4 %all-gather.26.cloned.1.call-done = bf16[1,768,3072]{2,1,0:T(8,128)(2,1)} async-done(((bf16[1,192,3072]{2,1,0:T(8,128)(2,1)}), bf16[1,768,3072]{2,1,0:T(8,128)(2,1)}) %all-gather.26.cloned.1.call-update) | async-done | bytes 4718608 | tf_op jit(solution)/shard_map/all_gather | solution.py:79
  229.3 89.8 %all-gather.28.cloned.1.call-done = bf16[1,768,3072]{2,1,0:T(8,128)(2,1)} async-done(((bf16[1,192,3072]{2,1,0:T(8,128)(2,1)}), bf16[1,768,3072]{2,1,0:T(8,128)(2,1)}) %all-gather.28.cloned.1.call-update) | async-done | bytes 4718608 | tf_op jit(solution)/shard_map/all_gather | solution.py:81
  319.1 9.6 fusion.11
  328.7 79.8 %all-gather.22.cloned.1.call-done = bf16[1,3072,768]{2,1,0:T(8,128)(2,1)} async-done(((bf16[1,768,768]{2,1,0:T(8,128)(2,1)}), bf16[1,3072,768]{2,1,0:T(8,128)(2,1)}) %all-gather.22.cloned.1.call-update) | async-done | bytes 4718608 | tf_op jit(solution)/shard_map/all_gather | solution.py:80
  408.5 89.4 %all-gather.24.cloned.1.call-done = bf16[1,3072,768]{2,1,0:T(8,128)(2,1)} async-done(((bf16[1,768,768]{2,1,0:T(8,128)(2,1)}), bf16[1,3072,768]{2,1,0:T(8,128)(2,1)}) %all-gather.24.cloned.1.call-update) | async-done | bytes 4718608 | tf_op jit(solution)/shard_map/all_gather | solution.py:82
  497.9 8.1 fusion.42
  510.7 13.1 %all-gather.4 = bf16[4,192,16]{1,2,0:T(8,128)(2,1)S(1)} all-gather(bf16[1,192,16]{1,2,0:T(8,128)(2,1)S(1)} %convert_bitcast_fusion), channel_id=1, replica_groups=mesh['dp'=4,'expert'=8] {'dp'}, dimensions={0}, use_global_device_ids=true | all-gather | bytes 30720 | tf_op jit(solution)/shard_map/all_gather | solution.py:72
  552.3 19.1 %all_to_all.21 = bf16[8,2,40,768]{3,2,1,0:T(8,128)(2,1)S(1)} all-to-all(bf16[8,2,40,768]{3,2,1,0:T(8,128)(2,1)S(1)} %multiply_convert_fusion), channel_id=1, replica_groups=mesh['dp'=4,'expert'=8] {'expert'}, dimensions={0} | all-to-all | bytes 1966080 | tf_op jit(solution)/shard_map/all_to_all | solution.py:190
  572.3 12.5 %fusion.7 = bf16[8,2,40,3072]{3,2,0,1:T(8,128)(2,1)} fusion(f32[2,3072,8,40]{1,3,2,0:T(8,128)} %get-tuple-element.49, bf16[1,3072,768]{2,1,0:T(8,128)(2,1)} %all-gather.24.cloned.1.call-done, bf16[1,3072,768]{2,1,0:T(8,128)(2,1)} %all-gather.22.cloned.1.call-done, bf16[8,2,40,768]{3,2,1,0:T(8,128)(2,1)S(1)} %all_to_all.21), kind=kOutput, calls=%fused_computation.19 | convolution fusion | flops 3078094848 | bytes 22216704 | tf_op jit(solution)/shard_map/sekd,efd->sekf/dot_general | solution.py:191
  584.8 6.9 fusion.41
  604.7 6.2 all-to-all-done.3
  630.5 4.9 fusion.56
  635.4 5.0 fusion.53
  649.0 6.6 bitcast_convert_fusion.1
  656.8 6.5 bitcast_convert_fusion
  670.7 38.8 %all-reduce.6 = (f32[768,16]{0,1:T(8,128)S(1)}, f32[768]{0:T(1024)S(1)}, f32[768]{0:T(1024)S(1)}, f32[768]{0:T(1024)S(1)}, f32[768]{0:T(1024)S(1)}) all-reduce(f32[768,16]{0,1:T(8,128)S(1)} %fusion.116, f32[768]{0:T(1024)S(1)} %get-tuple-element.15, ...), channel_id=1, replica_groups=mesh['dp'=4,'expert'=8] {'dp','expert'}, use_global_device_ids=true, to_apply=%region_27.28 | all-reduce | flops 15360 | bytes 122880 | tf_op jit(solution)/shard_map/psum | solution.py:278
  713.9 122.9 %all-reduce.11.cloned.1.call-done = (f32[768,768]{1,0:T(8,128)}, f32[768,768]{1,0:T(8,128)}, f32[768,768]{1,0:T(8,128)}, f32[768,768]{1,0:T(8,128)}) async-done(((f32[768,768]{1,0:T(8,128)}, f32[768,768]{1,0:T(8,128)}, f32[768,768]{1,0:T(8,128)}, f32[768,768]{1,0:T(8,128)}), (f32[768,768]{1,0:T(8,128)}, f32[768,768]{1,0:T(8,128)}, f32[768,768]{1,0:T(8,128)}, ...) | async-done | bytes 9437200 | tf_op jit(solution)/shard_map/psum | solution.py:278
  844.5 79.9 %reduce-scatter.3.cloned.1.call-done = bf16[192,3072]{1,0:T(8,128)(2,1)} async-done(((bf16[768,3072]{1,0:T(8,128)(2,1)}), bf16[192,3072]{1,0:T(8,128)(2,1)}) %reduce-scatter.3.cloned.1.call-update) | async-done | bytes 1179664 | tf_op jit(solution)/shard_map/reduce_scatter | solution.py:207
  927.2 85.2 %reduce-scatter.5.cloned.1.call-done = bf16[768,768]{1,0:T(8,128)(2,1)} async-done(((bf16[3072,768]{1,0:T(8,128)(2,1)}), bf16[768,768]{1,0:T(8,128)(2,1)}) %reduce-scatter.5.cloned.1.call-update) | async-done | bytes 1179664 | tf_op jit(solution)/shard_map/reduce_scatter | solution.py:210
  (322 shorter events, 140.4 us)
Async XLA Ops:
  7.2 38.8 %all-gather.14.cloned.1.call-start = ((), (), s32[]{:S(2)}) async-start(), calls=%async_computation.6 | async-start | bytes 1474560 | tf_op jit(solution)/shard_map/all_gather | solution.py:70
  9.2 66.2 %all-gather.18.cloned.1.call-start = ((), (), s32[]{:S(2)}) async-start(), calls=%async_computation.8 | async-start | bytes 1474560 | tf_op jit(solution)/shard_map/all_gather | solution.py:69
  11.1 96.0 %all-gather.16.cloned.1.call-start = ((), (), s32[]{:S(2)}) async-start(), calls=%async_computation.7 | async-start | bytes 1474560 | tf_op jit(solution)/shard_map/all_gather | solution.py:68
  13.0 125.6 %all-gather.20.cloned.1.call-start = ((), (), s32[]{:S(2)}) async-start(), calls=%async_computation.9 | async-start | bytes 1474560 | tf_op jit(solution)/shard_map/all_gather | solution.py:71
  13.8 215.4 %all-gather.26.cloned.1.call-start = ((), (), s32[]{:S(2)}) async-start(), calls=%async_computation.14 | async-start | bytes 5898240 | tf_op jit(solution)/shard_map/all_gather | solution.py:79
  15.1 304.0 %all-gather.28.cloned.1.call-start = ((), (), s32[]{:S(2)}) async-start(), calls=%async_computation.15 | async-start | bytes 5898240 | tf_op jit(solution)/shard_map/all_gather | solution.py:81
  18.1 390.3 %all-gather.22.cloned.1.call-start = ((), (), s32[]{:S(2)}) async-start(), calls=%async_computation.12 | async-start | bytes 5898240 | tf_op jit(solution)/shard_map/all_gather | solution.py:80
  19.4 478.5 %all-gather.24.cloned.1.call-start = ((), (), s32[]{:S(2)}) async-start(), calls=%async_computation.13 | async-start | bytes 5898240 | tf_op jit(solution)/shard_map/all_gather | solution.py:82
  42.3 64.8 %copy-start.40 = (f32[768]{0:T(1024)}, f32[768]{0:T(1024)S(1)}, u32[]{:S(2)}) copy-start(f32[768]{0:T(1024)S(1)} %convert_element_type.216) | copy-start | bytes 9220
  42.3 98.4 %copy-start.42 = (f32[768]{0:T(1024)}, f32[768]{0:T(1024)S(1)}, u32[]{:S(2)}) copy-start(f32[768]{0:T(1024)S(1)} %convert_element_type.238) | copy-start | bytes 9220
  45.4 97.2 %copy-start.49 = (s32[1024]{0:T(1024)}, s32[1024]{0:T(1024)S(1)}, u32[]{:S(2)}) copy-start(s32[1024]{0:T(1024)S(1)} %get-tuple-element.53) | copy-start | bytes 12292
  45.6 61.5 %copy-start.38 = (f32[256]{0:T(256)}, f32[256]{0:T(256)S(1)}, u32[]{:S(2)}) copy-start(f32[256]{0:T(256)S(1)} %broadcast_multiply_fusion.1) | copy-start | bytes 3076
  45.9 61.2 %copy-start.47 = (f32[256]{0:T(256)}, f32[256]{0:T(256)S(1)}, u32[]{:S(2)}) copy-start(f32[256]{0:T(256)S(1)} %fusion.88) | copy-start | bytes 3076
  46.0 63.1 %copy-start.33 = (pred[256,256]{0,1:T(8,128)(4,1)}, pred[256,256]{0,1:T(8,128)(4,1)S(1)}, u32[]{:S(2)}) copy-start(pred[256,256]{0,1:T(8,128)(4,1)S(1)} %fusion.70) | copy-start | bytes 196612
  48.0 62.3 %copy-start.23 = (bf16[256,768]{0,1:T(8,128)(2,1)}, bf16[256,768]{0,1:T(8,128)(2,1)S(1)}, u32[]{:S(2)}) copy-start(bf16[256,768]{0,1:T(8,128)(2,1)S(1)} %copy.85) | copy-start | bytes 1179652
  163.8 164.9 %copy-start.26 = (bf16[8,2,40,768]{3,2,1,0:T(8,128)(2,1)}, bf16[8,2,40,768]{3,2,1,0:T(8,128)(2,1)S(1)}, u32[]{:S(2)}) copy-start(bf16[8,2,40,768]{3,2,1,0:T(8,128)(2,1)S(1)} %all_to_all.20) | copy-start | bytes 2949124
  507.1 27.5 %all-to-all-start.1 = ((bf16[8,2,40,768]{3,2,1,0:T(8,128)(2,1)}), bf16[8,2,40,768]{3,2,1,0:T(8,128)(2,1)S(1)}, u32[]{:S(2)}, u32[]{:S(2)}) async-start(bf16[8,2,40,768]{3,2,1,0:T(8,128)(2,1)} %copy.94), calls=%async_computation.1 | async-start | bytes 1966080 | tf_op jit(solution)/shard_map/all_to_all | solution.py:165
  592.8 18.2 %all-to-all-start.3 = ((bf16[8,2,40,768]{3,2,1,0:T(8,128)(2,1)}), bf16[8,2,40,768]{3,2,1,0:T(8,128)(2,1)S(1)}, u32[]{:S(2)}, u32[]{:S(2)}) async-start(bf16[8,2,40,768]{3,2,1,0:T(8,128)(2,1)} %copy.100), calls=%async_computation.3 | async-start | bytes 1966080 | tf_op jit(solution)/shard_map/all_to_all | solution.py:214
  596.4 240.4 %all-reduce.11.cloned.1.call-start = ((), (), s32[]{:S(2)}) async-start(), calls=%async_computation.16 | async-start | bytes 18874368 | tf_op jit(solution)/shard_map/psum | solution.py:278
  647.8 276.5 %reduce-scatter.3.cloned.1.call-start = ((), (), s32[]{:S(2)}) async-start(), calls=%async_computation.10 | async-start | bytes 5898240 | tf_op jit(solution)/shard_map/reduce_scatter | solution.py:207
  655.6 356.9 %reduce-scatter.5.cloned.1.call-start = ((), (), s32[]{:S(2)}) async-start(), calls=%async_computation.11 | async-start | bytes 5898240 | tf_op jit(solution)/shard_map/reduce_scatter | solution.py:210
  668.2 44.6 %copy-start.4 = (f32[256,768]{1,0:T(8,128)S(1)}, f32[256,768]{1,0:T(8,128)}, u32[]{:S(2)}) copy-start(f32[256,768]{1,0:T(8,128)} %copy-done.3) | copy-start | bytes 2359300
  668.2 44.6 %copy-start.7 = (bf16[256,768]{1,0:T(8,128)(2,1)S(1)}, bf16[256,768]{1,0:T(8,128)(2,1)}, u32[]{:S(2)}) copy-start(bf16[256,768]{1,0:T(8,128)(2,1)} %param.33) | copy-start | bytes 1179652
  668.2 44.6 %copy-start.59 = (f32[256]{0:T(256)S(1)}, f32[256]{0:T(256)}, u32[]{:S(2)}) copy-start(f32[256]{0:T(256)} %copy-done.58) | copy-start | bytes 3076
  (70 other events, 482.3 us)
Sparse Core Ops, SparseCore 0:
  10.1 33.5 all-gather.13
  45.8 29.5 all-gather.17
  77.6 29.4 all-gather.15
  109.1 29.4 all-gather.19
  140.6 88.6 all-gather.25
  231.3 87.7 all-gather.27
  320.7 87.7 all-gather.21
  410.1 87.7 all-gather.23
  647.9 188.8 all-reduce.10
  838.9 85.3 reduce-scatter.2
  926.6 85.7 reduce-scatter.4
where the time goes:
time: 1030 us; the launch traced here: 1020 us
  waiting for transfers between devices  702 us (68%)
  blocking collectives  104 us (10%)
  matrix products  91.2 us (9%)
  local copies, waits for them, and re-layouts  61 us (6%)
  other arithmetic  40.4 us (4%)
  between operations  15.9 us (2%)
    psum x1, waiting for transfers between devices, shards(): lax.psum((grad_query, grad_key, grad_value, grad_output, grad_router, gra...  123 us
    all_gather x1, waiting for transfers between devices, shards(): lax.all_gather(new_in[0].astype(jnp.bfloat16), 'dp', axis=0, tiled=True)  89.8 us
    all_gather x1, waiting for transfers between devices, shards(): lax.all_gather(new_out[0].astype(jnp.bfloat16), 'dp', axis=0, tiled=True)  89.4 us
    reduce_scatter x1, waiting for transfers between devices, shards(): lax.psum_scatter(grad_out_full.astype(jnp.bfloat16), 'dp', scatter_dimens...  85.2 us
    reduce_scatter x1, waiting for transfers between devices, shards(): lax.psum_scatter(grad_in_full.astype(jnp.bfloat16), 'dp', scatter_dimensi...  79.9 us
    all_gather x1, waiting for transfers between devices, shards(): lax.all_gather(frozen_out[0].astype(jnp.bfloat16), 'dp', axis=0, tiled=True)  79.8 us
    all_gather x1, waiting for transfers between devices, shards(): lax.all_gather(frozen_in[0].astype(jnp.bfloat16), 'dp', axis=0, tiled=True)  65.4 us
    psum x1, blocking collectives, shards(): lax.psum((grad_query, grad_key, grad_value, grad_output, grad_router, gra...  38.8 us
  transfers between devices with their start and end apart: 13, of which 11 were waited for; matrix products, arithmetic and copies ran while one was open for 9% of the time, Pallas kernels for 0%

commit v1 on v0

--- a/solution.py
+++ b/solution.py
@@ -7,6 +7,28 @@
 HEAD = 64
 NORM_EPS = 1e-05
 MASKED = -1e30
+
+
+def laid_out(blocks, dim):
+    shape = list(blocks.shape[1:])
+    shape[dim] *= blocks.shape[0]
+    return jnp.moveaxis(blocks, 0, dim).reshape(shape)
+
+
+def doubled(x, axis):
+    size = lax.axis_size(axis)
+    tiles = x[None]
+    for level in range(size.bit_length() - 1):
+        stride = 1 << level
+        received = lax.ppermute(tiles, axis, [(i, i ^ stride) for i in range(size)])
+        both = jnp.stack([tiles, received])
+        upper = lax.axis_index(axis) >> level & 1
+        tiles = jnp.where(upper == 0, both, both[::-1]).reshape(-1, *x.shape)
+    return tiles
+
+
+def doubled_up(array, axis, dim):
+    return laid_out(doubled(array, axis), dim)
 
 
 def layer_norm(values, norm_gain, norm_shift):
@@ -77,7 +99,7 @@
     )
     full_frozen_in, full_frozen_out, full_new_in, full_new_out = (
         lax.all_gather(frozen_in[0].astype(jnp.bfloat16), "dp", axis=0, tiled=True),
-        lax.all_gather(frozen_out[0].astype(jnp.bfloat16), "dp", axis=0, tiled=True),
+        doubled_up(frozen_out[0].astype(jnp.bfloat16), "dp", 0),
         lax.all_gather(new_in[0].astype(jnp.bfloat16), "dp", axis=0, tiled=True),
         lax.all_gather(new_out[0].astype(jnp.bfloat16), "dp", axis=0, tiled=True),
     )

time: 1030 us -> 1060 us (1.029)
  waiting for transfers between devices: 702 us -> 735 us
  starting transfers between devices: 7.68 us -> 20.2 us
  blocking collectives: 104 us -> 91.7 us
  local copies, waits for them, and re-layouts: 61 us -> 49.5 us
    all_gather x1, waiting for transfers between devices: 79.8 us -> 39.7 us  [shards(): lax.all_gather(frozen_out[0].astype(jnp.bfloat16), 'dp', axis=0, tiled=True)]
    all_gather x1, waiting for transfers between devices: 27.4 us -> 67.2 us  [shards(): lax.all_gather(w_key.astype(jnp.bfloat16), 'dp', axis=0, tiled=True)]
    all_gather x1, waiting for transfers between devices: 0.02 us -> 39.1 us  [shards(): lax.all_gather(w_value.astype(jnp.bfloat16), 'dp', axis=0, tiled=True)]
    all_to_all x2 -> x0, blocking collectives: 37.4 us -> none  [the longest x1 19.1 us: shards(): lax.all_to_all(d_send, 'expert', split_axis=0, concat_axis=0, tiled=True)]
    all_gather x1, waiting for transfers between devices: 29.7 us -> 0.01 us  [shards(): lax.all_gather(w_query.astype(jnp.bfloat16), 'dp', axis=0, tiled=True)]
    unnamed x1, blocking collectives: 14.3 us -> 38.3 us
    all_gather x1, waiting for transfers between devices: 26.4 us -> 49.3 us  [shards(): lax.all_gather(w_output.astype(jnp.bfloat16), 'dp', axis=0, tiled=True)]
  transfers between devices with their start and end apart: 13 -> 17, of which waited for: 11 -> 12; matrix products, arithmetic and copies ran while one was open for 9% -> 12% of each run, Pallas kernels for 0% -> 0%
where the time goes in v1:
time: 1060 us; the launch traced here: 1050 us
  waiting for transfers between devices  735 us (69%)
  matrix products  93.1 us (9%)
  blocking collectives  91.7 us (9%)
  local copies, waits for them, and re-layouts  49.5 us (5%)
  other arithmetic  48.2 us (5%)
  starting transfers between devices  20.2 us (2%)
  between operations  15.9 us (2%)
    psum x1, waiting for transfers between devices, shards(): lax.psum((grad_query, grad_key, grad_value, grad_output, grad_router, gra...  124 us
    all_gather x1, waiting for transfers between devices, shards(): lax.all_gather(new_in[0].astype(jnp.bfloat16), 'dp', axis=0, tiled=True)  89.3 us
    reduce_scatter x1, waiting for transfers between devices, shards(): lax.psum_scatter(grad_in_full.astype(jnp.bfloat16), 'dp', scatter_dimensi...  85.3 us
    reduce_scatter x1, waiting for transfers between devices, shards(): lax.psum_scatter(grad_out_full.astype(jnp.bfloat16), 'dp', scatter_dimens...  79.9 us
    all_gather x1, waiting for transfers between devices, shards(): lax.all_gather(new_out[0].astype(jnp.bfloat16), 'dp', axis=0, tiled=True)  79.6 us
    all_gather x1, waiting for transfers between devices, shards(): lax.all_gather(w_key.astype(jnp.bfloat16), 'dp', axis=0, tiled=True)  67.2 us
    all_gather x1, waiting for transfers between devices, shards(): lax.all_gather(frozen_in[0].astype(jnp.bfloat16), 'dp', axis=0, tiled=True)  65 us
    all_gather x1, waiting for transfers between devices, shards(): lax.all_gather(w_output.astype(jnp.bfloat16), 'dp', axis=0, tiled=True)  49.3 us
  transfers between devices with their start and end apart: 17, of which 12 were waited for; matrix products, arithmetic and copies ran while one was open for 12% of the time, Pallas kernels for 0%

profile of v1, /device:TPU:0, one launch (start us, length us, event | category | flops | bytes accessed | tf_op | source)
XLA Modules:
  0.0 1053.8 jit_solution(1341494153366915793)
XLA Ops:
  33.7 38.3 %all-reduce.8 = (bf16[768]{0:T(1024)(128)(2,1)S(1)}, bf16[768]{0:T(1024)(128)(2,1)S(1)}, bf16[768]{0:T(1024)(128)(2,1)S(1)}, bf16[768]{0:T(1024)(128)(2,1)S(1)}) all-reduce(bf16[768]{0:T(1024)(128)(2,1)S(1)} %dynamic-update-slice.1, bf16[768]{0:T(1024)(128)(2,1)S(1)} %dynamic-update-slice, ...), channel_id=1, replica_groups=mesh['dp'=4,'expert'=8] {'dp'}, use_global_device_ids=true, to_apply=%add.3 | all-reduce | flops 3072 | bytes 12288
  78.8 67.2 %all-gather.18.cloned.1.call-done = bf16[768,768]{1,0:T(8,128)(2,1)} async-done(((bf16[192,768]{1,0:T(8,128)(2,1)}), bf16[768,768]{1,0:T(8,128)(2,1)}) %all-gather.18.cloned.1.call-update) | async-done | bytes 1179664 | tf_op jit(solution)/shard_map/all_gather | solution.py:91
  148.0 39.1 %all-gather.14.cloned.1.call-done = bf16[768,768]{1,0:T(8,128)(2,1)} async-done(((bf16[192,768]{1,0:T(8,128)(2,1)}), bf16[768,768]{1,0:T(8,128)(2,1)}) %all-gather.14.cloned.1.call-update) | async-done | bytes 1179664 | tf_op jit(solution)/shard_map/all_gather | solution.py:92
  192.2 49.3 %all-gather.20.cloned.1.call-done = bf16[768,768]{1,0:T(8,128)(2,1)} async-done(((bf16[192,768]{1,0:T(8,128)(2,1)}), bf16[768,768]{1,0:T(8,128)(2,1)}) %all-gather.20.cloned.1.call-update) | async-done | bytes 1179664 | tf_op jit(solution)/shard_map/all_gather | solution.py:93
  258.1 8.5 all-to-all-done
  266.5 65.0 %all-gather.24.cloned.1.call-done = bf16[1,768,3072]{2,1,0:T(8,128)(2,1)} async-done(((bf16[1,192,3072]{2,1,0:T(8,128)(2,1)}), bf16[1,768,3072]{2,1,0:T(8,128)(2,1)}) %all-gather.24.cloned.1.call-update) | async-done | bytes 4718608 | tf_op jit(solution)/shard_map/all_gather | solution.py:101
  331.6 89.3 %all-gather.26.cloned.1.call-done = bf16[1,768,3072]{2,1,0:T(8,128)(2,1)} async-done(((bf16[1,192,3072]{2,1,0:T(8,128)(2,1)}), bf16[1,768,3072]{2,1,0:T(8,128)(2,1)}) %all-gather.26.cloned.1.call-update) | async-done | bytes 4718608 | tf_op jit(solution)/shard_map/all_gather | solution.py:103
  420.8 9.8 fusion.19
  430.6 79.6 %all-gather.22.cloned.1.call-done = bf16[1,3072,768]{2,1,0:T(8,128)(2,1)} async-done(((bf16[1,768,768]{2,1,0:T(8,128)(2,1)}), bf16[1,3072,768]{2,1,0:T(8,128)(2,1)}) %all-gather.22.cloned.1.call-update) | async-done | bytes 4718608 | tf_op jit(solution)/shard_map/all_gather | solution.py:104
  510.2 8.1 fusion.53
  527.7 13.7 %all-gather.4 = bf16[4,192,16]{1,2,0:T(8,128)(2,1)S(1)} all-gather(bf16[1,192,16]{1,2,0:T(8,128)(2,1)S(1)} %convert_bitcast_fusion), channel_id=1, replica_groups=mesh['dp'=4,'expert'=8] {'dp'}, dimensions={0}, use_global_device_ids=true | all-gather | bytes 30720 | tf_op jit(solution)/shard_map/all_gather | solution.py:94
  555.0 5.4 all-to-all-start.2
  560.4 39.7 %all-gather.28.cloned.1.call-done = bf16[1,3072,768]{2,1,0:T(8,128)(2,1)} async-done(((bf16[1,768,768]{2,1,0:T(8,128)(2,1)}), bf16[1,3072,768]{2,1,0:T(8,128)(2,1)}) %all-gather.28.cloned.1.call-update) | async-done | bytes 4718608 | tf_op jit(solution)/shard_map/all_gather | solution.py:206
  600.1 11.5 %fusion.15 = bf16[8,2,40,3072]{3,2,0,1:T(8,128)(2,1)S(1)} fusion(f32[2,3072,8,40]{1,3,2,0:T(8,128)} %get-tuple-element.51, bf16[1,3072,768]{2,1,0:T(8,128)(2,1)} %all-gather.22.cloned.1.call-done, bf16[1,3072,768]{2,1,0:T(8,128)(2,1)} %all-gather.28.cloned.1.call-done, bf16[8,2,40,768]{3,2,1,0:T(8,128)(2,1)S(1)} %all-to-all-done.2), kind=kOutput, calls=%fused_computation.26 | convolution fusion | flops 3078094848 | bytes 22216704 | tf_op jit(solution)/shard_map/sekd,efd->sekf/dot_general | solution.py:213
  611.6 8.5 fusion.56
  631.6 7.9 all-to-all-done.3
  659.8 5.0 fusion.67
  664.8 4.9 fusion.70
  679.6 6.4 bitcast_convert_fusion
  686.1 6.6 bitcast_convert_fusion.1
  700.1 39.7 %all-reduce.6 = (f32[768,16]{0,1:T(8,128)S(1)}, f32[768]{0:T(1024)S(1)}, f32[768]{0:T(1024)S(1)}, f32[768]{0:T(1024)S(1)}, f32[768]{0:T(1024)S(1)}) all-reduce(f32[768,16]{0,1:T(8,128)S(1)} %fusion.130, f32[768]{0:T(1024)S(1)} %get-tuple-element.15, ...), channel_id=1, replica_groups=mesh['dp'=4,'expert'=8] {'dp','expert'}, use_global_device_ids=true, to_apply=%region_27.28 | all-reduce | flops 15360 | bytes 122880 | tf_op jit(solution)/shard_map/psum | solution.py:300
  744.1 124.4 %all-reduce.11.cloned.1.call-done = (f32[768,768]{1,0:T(8,128)}, f32[768,768]{1,0:T(8,128)}, f32[768,768]{1,0:T(8,128)}, f32[768,768]{1,0:T(8,128)}) async-done(((f32[768,768]{1,0:T(8,128)}, f32[768,768]{1,0:T(8,128)}, f32[768,768]{1,0:T(8,128)}, f32[768,768]{1,0:T(8,128)}), (f32[768,768]{1,0:T(8,128)}, f32[768,768]{1,0:T(8,128)}, f32[768,768]{1,0:T(8,128)}, ...) | async-done | bytes 9437200 | tf_op jit(solution)/shard_map/psum | solution.py:300
  876.2 79.9 %reduce-scatter.5.cloned.1.call-done = bf16[768,768]{1,0:T(8,128)(2,1)} async-done(((bf16[3072,768]{1,0:T(8,128)(2,1)}), bf16[768,768]{1,0:T(8,128)(2,1)}) %reduce-scatter.5.cloned.1.call-update) | async-done | bytes 1179664 | tf_op jit(solution)/shard_map/reduce_scatter | solution.py:232
  958.9 85.3 %reduce-scatter.3.cloned.1.call-done = bf16[192,3072]{1,0:T(8,128)(2,1)} async-done(((bf16[768,3072]{1,0:T(8,128)(2,1)}), bf16[192,3072]{1,0:T(8,128)(2,1)}) %reduce-scatter.3.cloned.1.call-update) | async-done | bytes 1179664 | tf_op jit(solution)/shard_map/reduce_scatter | solution.py:229
  (296 shorter events, 145.0 us)
Async XLA Ops:
  7.2 69.6 %all-gather.16.cloned.1.call-start = ((), (), s32[]{:S(2)}) async-start(), calls=%async_computation.7 | async-start | bytes 1474560 | tf_op jit(solution)/shard_map/all_gather | solution.py:90
  9.2 136.8 %all-gather.18.cloned.1.call-start = ((), (), s32[]{:S(2)}) async-start(), calls=%async_computation.8 | async-start | bytes 1474560 | tf_op jit(solution)/shard_map/all_gather | solution.py:91
  11.1 176.0 %all-gather.14.cloned.1.call-start = ((), (), s32[]{:S(2)}) async-start(), calls=%async_computation.6 | async-start | bytes 1474560 | tf_op jit(solution)/shard_map/all_gather | solution.py:92
  13.0 228.5 %all-gather.20.cloned.1.call-start = ((), (), s32[]{:S(2)}) async-start(), calls=%async_computation.9 | async-start | bytes 1474560 | tf_op jit(solution)/shard_map/all_gather | solution.py:93
  13.8 317.7 %all-gather.24.cloned.1.call-start = ((), (), s32[]{:S(2)}) async-start(), calls=%async_computation.13 | async-start | bytes 5898240 | tf_op jit(solution)/shard_map/all_gather | solution.py:101
  15.1 405.7 %all-gather.26.cloned.1.call-start = ((), (), s32[]{:S(2)}) async-start(), calls=%async_computation.14 | async-start | bytes 5898240 | tf_op jit(solution)/shard_map/all_gather | solution.py:103
  18.1 492.1 %all-gather.22.cloned.1.call-start = ((), (), s32[]{:S(2)}) async-start(), calls=%async_computation.12 | async-start | bytes 5898240 | tf_op jit(solution)/shard_map/all_gather | solution.py:104
  21.3 578.8 %all-gather.28.cloned.1.call-start = ((), (), s32[]{:S(2)}) async-start(), calls=%async_computation.15 | async-start | bytes 5898240 | tf_op jit(solution)/shard_map/all_gather | solution.py:206
  22.5 50.1 %collective-permute-start = (bf16[1,768,768]{2,1,0:T(8,128)(2,1)}, bf16[1,768,768]{2,1,0:T(8,128)(2,1)}, u32[]{:S(2)}, u32[]{:S(2)}) collective-permute-start(bf16[1,768,768]{2,1,0:T(8,128)(2,1)} %convert_element_type.240), channel_id=1, source_target_pairs={{0,8},{8,0},{16,24},{24,16},{1,9},{9,1},{17,25},{25,17},{2,10},{10... | collective-permute-start | bytes 3538952 | tf_op jit(solution)/shard_map/ppermute | solution.py:23
  27.8 513.8 %copy-start.36 = (s32[512]{0:T(512)}, s32[512]{0:T(512)S(1)}, u32[]{:S(2)}) copy-start(s32[512]{0:T(512)S(1)} %fusion.89) | copy-start | bytes 6148
  72.0 115.1 %copy-start.29 = (f32[768]{0:T(1024)}, f32[768]{0:T(1024)S(1)}, u32[]{:S(2)}) copy-start(f32[768]{0:T(1024)S(1)} %convert_element_type.227) | copy-start | bytes 9220
  72.0 171.6 %copy-start.31 = (f32[768]{0:T(1024)}, f32[768]{0:T(1024)S(1)}, u32[]{:S(2)}) copy-start(f32[768]{0:T(1024)S(1)} %convert_element_type.249) | copy-start | bytes 9220
  72.3 114.8 %copy-start.34 = (f32[256]{0:T(256)}, f32[256]{0:T(256)S(1)}, u32[]{:S(2)}) copy-start(f32[256]{0:T(256)S(1)} %fusion.102) | copy-start | bytes 3076
  72.5 116.6 %copy-start.27 = (pred[256,256]{0,1:T(8,128)(4,1)}, pred[256,256]{0,1:T(8,128)(4,1)S(1)}, u32[]{:S(2)}) copy-start(pred[256,256]{0,1:T(8,128)(4,1)S(1)} %fusion.84) | copy-start | bytes 196612
  76.8 175.2 %collective-permute-start.1 = (bf16[2,768,768]{2,1,0:T(8,128)(2,1)}, bf16[2,768,768]{2,1,0:T(8,128)(2,1)}, u32[]{:S(2)}, u32[]{:S(2)}) collective-permute-start(bf16[2,768,768]{2,1,0:T(8,128)(2,1)} %get-tuple-element.40), channel_id=1, source_target_pairs={{0,16},{8,24},{16,0},{24,8},{1,17},{9,25},{17,1},{25,9},{2,18},{10... | collective-permute-start | bytes 7077896 | tf_op jit(solution)/shard_map/ppermute | solution.py:23
  78.8 110.3 %copy-start.21 = (bf16[256,768]{0,1:T(8,128)(2,1)}, bf16[256,768]{0,1:T(8,128)(2,1)S(1)}, u32[]{:S(2)}) copy-start(bf16[256,768]{0,1:T(8,128)(2,1)S(1)} %copy.86) | copy-start | bytes 1179652
  248.0 18.5 %all-to-all-start = ((bf16[8,2,40,768]{3,2,1,0:T(8,128)(2,1)}), bf16[8,2,40,768]{3,2,1,0:T(8,128)(2,1)S(1)}, u32[]{:S(2)}, u32[]{:S(2)}) async-start(bf16[8,2,40,768]{3,2,1,0:T(8,128)(2,1)} %bitcast.20), calls=%async_computation | async-start | bytes 1966080 | tf_op jit(solution)/shard_map/all_to_all | solution.py:179
  266.5 164.0 %copy-start.24 = (bf16[8,2,40,768]{3,2,1,0:T(8,128)(2,1)}, bf16[8,2,40,768]{3,2,1,0:T(8,128)(2,1)S(1)}, u32[]{:S(2)}) copy-start(bf16[8,2,40,768]{3,2,1,0:T(8,128)(2,1)S(1)} %all-to-all-done) | copy-start | bytes 2949124
  519.3 26.3 %all-to-all-start.1 = ((bf16[8,2,40,768]{3,2,1,0:T(8,128)(2,1)}), bf16[8,2,40,768]{3,2,1,0:T(8,128)(2,1)S(1)}, u32[]{:S(2)}, u32[]{:S(2)}) async-start(bf16[8,2,40,768]{3,2,1,0:T(8,128)(2,1)} %copy.94), calls=%async_computation.1 | async-start | bytes 1966080 | tf_op jit(solution)/shard_map/all_to_all | solution.py:187
  555.0 45.1 %all-to-all-start.2 = ((bf16[8,2,40,768]{3,2,1,0:T(8,128)(2,1)}), bf16[8,2,40,768]{3,2,1,0:T(8,128)(2,1)S(1)}, u32[]{:S(2)}, u32[]{:S(2)}) async-start(bf16[8,2,40,768]{3,2,1,0:T(8,128)(2,1)} %multiply_convert_fusion), calls=%async_computation.2 | async-start | bytes 1966080 | tf_op jit(solution)/shard_map/all_to_all | solution.py:212
  621.2 18.3 %all-to-all-start.3 = ((bf16[8,2,40,768]{3,2,1,0:T(8,128)(2,1)}), bf16[8,2,40,768]{3,2,1,0:T(8,128)(2,1)S(1)}, u32[]{:S(2)}, u32[]{:S(2)}) async-start(bf16[8,2,40,768]{3,2,1,0:T(8,128)(2,1)} %copy.100), calls=%async_computation.3 | async-start | bytes 1966080 | tf_op jit(solution)/shard_map/all_to_all | solution.py:236
  624.8 243.7 %all-reduce.11.cloned.1.call-start = ((), (), s32[]{:S(2)}) async-start(), calls=%async_computation.16 | async-start | bytes 18874368 | tf_op jit(solution)/shard_map/psum | solution.py:300
  679.3 276.7 %reduce-scatter.5.cloned.1.call-start = ((), (), s32[]{:S(2)}) async-start(), calls=%async_computation.11 | async-start | bytes 5898240 | tf_op jit(solution)/shard_map/reduce_scatter | solution.py:232
  686.0 358.2 %reduce-scatter.3.cloned.1.call-start = ((), (), s32[]{:S(2)}) async-start(), calls=%async_computation.10 | async-start | bytes 5898240 | tf_op jit(solution)/shard_map/reduce_scatter | solution.py:229
  (56 other events, 517.9 us)
Sparse Core Ops, SparseCore 0:
  10.1 43.7 all-gather.15
  56.1 89.8 all-gather.17
  148.2 38.8 all-gather.13
  189.1 52.3 all-gather.19
  242.9 88.6 all-gather.23
  333.0 87.7 all-gather.25
  422.4 87.7 all-gather.21
  511.8 88.2 all-gather.27
  679.5 189.0 all-reduce.10
  870.7 85.3 reduce-scatter.4
  958.3 85.7 reduce-scatter.2
